TPU v7x, 32 devices: a whole 2x2x4 slice. The times are simulated.
32 devices in a mesh: dp: 2 (over core), ctx: 16 (over z, y, x).
Axes of the slice: x: 2, y: 2, z: 4, core: 2. Of those that a mesh axis runs over, the one named last changes fastest.
Arguments:
- layer_in: bfloat16 [2, 4096, 768], P('dp', 'ctx'), may hold values from -6 to 6
- out_grad: bfloat16 [2, 4096, 768], P('dp', 'ctx'), may hold values from -6 to 6
- first_gain: bfloat16 [768], P('dp'), may hold values from 0.099609375 to 1.8984375
- query_weight: bfloat16 [768, 768], P('dp'), may hold values from -0.21875 to 0.21875
- key_weight: bfloat16 [768, 768], P('dp'), may hold values from -0.21875 to 0.21875
- value_weight: bfloat16 [768, 768], P('dp'), may hold values from -0.21875 to 0.21875
- output_weight: bfloat16 [768, 768], P('dp'), may hold values from -6 to 6
- second_gain: bfloat16 [768], P('dp'), may hold values from 0.099609375 to 1.8984375
- gate_weight: bfloat16 [768, 2048], P('dp'), may hold values from -0.21875 to 0.21875
- up_weight: bfloat16 [768, 2048], P('dp'), may hold values from -0.21875 to 0.21875
- down_weight: bfloat16 [2048, 768], P('dp'), may hold values from -0.125 to 0.125
Outputs:
- layer_out: bfloat16 [2, 4096, 768], P('dp', 'ctx')
- in_grad: bfloat16 [2, 4096, 768], P('dp', 'ctx')
- first_gain_grad: float32 [768], P('dp')
- query_grad: float32 [768, 768], P('dp')
- key_grad: float32 [768, 768], P('dp')
- value_grad: float32 [768, 768], P('dp')
- output_grad: float32 [768, 768], P('dp')
- second_gain_grad: float32 [768], P('dp')
- gate_grad: float32 [768, 2048], P('dp')
- up_grad: float32 [768, 2048], P('dp')
- down_grad: float32 [2048, 768], P('dp')
All inputs are finite; a program needn't handle non-finite values.
Results may differ from a plain program's by a relative error of at most 0.02.
Values may be sent and summed in bfloat16 or wider, within the bound.
No kernel may reach another device: no remote copies, remote signals or barrier semaphores. Data moves between devices by JAX's collectives and lax.ppermute only.
A program may use at most 448 MiB of HBM per device.

v0:
```python
import jax
import jax.numpy as jnp
from jax import lax
from jax.sharding import PartitionSpec as P

HEADS = 12
HEAD_DIM = 64


EPS = 1e-06


def normed(rows, gain):
    return rows * lax.rsqrt(jnp.mean(rows * rows, axis=-1, keepdims=True) + EPS) * gain


def gated(gate, upper):
    return jax.nn.gelu(gate, approximate=True) * upper


def heads_of(rows):
    return rows.reshape(rows.shape[0], HEADS, HEAD_DIM)


def scores_of(query, keys):
    return jnp.einsum(
        "qhd,khd->hqk", heads_of(query), heads_of(keys), preferred_element_type=jnp.float32
    ) * HEAD_DIM ** (-0.5)


def attend(operands):
    query, keys, values = operands
    scores = scores_of(query, keys)
    top = jnp.max(scores, axis=-1, keepdims=True)
    expd = jnp.exp(scores - top)
    total = jnp.sum(expd, axis=-1, keepdims=True)
    probs = (expd / total).astype(jnp.bfloat16)
    mixed = jnp.einsum("hqk,khd->qhd", probs, heads_of(values), preferred_element_type=jnp.float32)
    mixed = mixed.reshape(query.shape[0], HEADS * HEAD_DIM).astype(jnp.bfloat16)
    return (mixed, (top + jnp.log(total))[..., 0])


def back_core(query, keys, values, grad_mix, logsum):
    probs = jnp.exp(scores_of(query, keys) - logsum[..., None])
    grad_prob = jnp.einsum(
        "qhd,khd->hqk", heads_of(grad_mix), heads_of(values), preferred_element_type=jnp.float32
    )
    delta = jnp.sum(grad_prob * probs, axis=-1)
    grad_score = (probs * (grad_prob - delta[..., None])).astype(jnp.bfloat16)
    return (probs, grad_score, delta)


def query_part(grad_score, keys, count):
    grad_query = jnp.einsum(
        "hqk,khd->qhd", grad_score, heads_of(keys), preferred_element_type=jnp.float32
    ) * HEAD_DIM ** (-0.5)
    return grad_query.reshape(count, HEADS * HEAD_DIM).astype(jnp.bfloat16)


def attend_back(operands):
    query, keys, values, grad_mix, logsum = operands
    probs, grad_score, delta = back_core(query, keys, values, grad_mix, logsum)
    grad_query = query_part(grad_score, keys, query.shape[0])
    grad_keys = jnp.einsum(
        "hqk,qhd->khd", grad_score, heads_of(query), preferred_element_type=jnp.float32
    ) * HEAD_DIM ** (-0.5)
    grad_values = jnp.einsum(
        "hqk,qhd->khd",
        probs.astype(jnp.bfloat16),
        heads_of(grad_mix),
        preferred_element_type=jnp.float32,
    )
    return (
        grad_query,
        grad_keys.reshape(keys.shape[0], -1),
        grad_values.reshape(keys.shape[0], -1),
    )


def product(left, right):
    return jnp.dot(left, right, preferred_element_type=jnp.float32)


def on_device(
    layer_in,
    out_grad,
    first_gain,
    query_weight,
    key_weight,
    value_weight,
    output_weight,
    second_gain,
    gate_weight,
    up_weight,
    down_weight,
):
    seqs, local, width = layer_in.shape
    rows = seqs * local

    def shaped(matrix):
        return matrix.reshape(seqs, local, width)

    gain_one, w_query, w_key, w_value, w_output = (
        lax.all_gather(first_gain, "dp", axis=0, tiled=True),
        lax.all_gather(query_weight, "dp", axis=0, tiled=True),
        lax.all_gather(key_weight, "dp", axis=0, tiled=True),
        lax.all_gather(value_weight, "dp", axis=0, tiled=True),
        lax.all_gather(output_weight, "dp", axis=0, tiled=True),
    )
    inputs = layer_in.reshape(rows, width).astype(jnp.float32)
    gain_one_f = gain_one.astype(jnp.float32)
    normal_one = normed(inputs, gain_one_f).astype(jnp.bfloat16)
    query = product(normal_one, w_query).astype(jnp.bfloat16)
    keys = product(normal_one, w_key).astype(jnp.bfloat16)
    values = product(normal_one, w_value).astype(jnp.bfloat16)
    keys_all, values_all = (
        lax.all_gather(shaped(keys), "ctx", axis=1, tiled=True),
        lax.all_gather(shaped(values), "ctx", axis=1, tiled=True),
    )
    mixed, logsum = lax.map(attend, (shaped(query), keys_all, values_all))
    mixed_rows = mixed.reshape(rows, width)
    middle = inputs + product(mixed_rows, w_output)
    gain_two, w_gate, w_up, w_down = (
        lax.all_gather(second_gain, "dp", axis=0, tiled=True),
        lax.all_gather(gate_weight, "dp", axis=0, tiled=True),
        lax.all_gather(up_weight, "dp", axis=0, tiled=True),
        lax.all_gather(down_weight, "dp", axis=0, tiled=True),
    )
    gain_two_f = gain_two.astype(jnp.float32)
    normal_two = normed(middle, gain_two_f).astype(jnp.bfloat16)
    gate = product(normal_two, w_gate)
    upper = product(normal_two, w_up)
    hidden = gated(gate, upper).astype(jnp.bfloat16)
    result = middle + product(hidden, w_down)
    layer_out = result.astype(jnp.bfloat16).reshape(seqs, local, width)
    gain_one, w_query, w_key, w_value, w_output = (
        lax.all_gather(first_gain, "dp", axis=0, tiled=True),
        lax.all_gather(query_weight, "dp", axis=0, tiled=True),
        lax.all_gather(key_weight, "dp", axis=0, tiled=True),
        lax.all_gather(value_weight, "dp", axis=0, tiled=True),
        lax.all_gather(output_weight, "dp", axis=0, tiled=True),
    )
    gain_two, w_gate, w_up, w_down = (
        lax.all_gather(second_gain, "dp", axis=0, tiled=True),
        lax.all_gather(gate_weight, "dp", axis=0, tiled=True),
        lax.all_gather(up_weight, "dp", axis=0, tiled=True),
        lax.all_gather(down_weight, "dp", axis=0, tiled=True),
    )
    gain_one_f = gain_one.astype(jnp.float32)
    gain_two_f = gain_two.astype(jnp.float32)
    grad_rows = out_grad.reshape(rows, width)
    grad_down = product(hidden.T, grad_rows)
    grad_hidden = product(grad_rows, w_down.T)
    unused, gate_back = jax.vjp(gated, gate, upper)
    grad_gate, grad_upper = gate_back(grad_hidden)
    grad_gate = grad_gate.astype(jnp.bfloat16)
    grad_upper = grad_upper.astype(jnp.bfloat16)
    grad_wgate = product(normal_two.T, grad_gate)
    grad_wup = product(normal_two.T, grad_upper)
    grad_normal_two = product(grad_gate, w_gate.T) + product(grad_upper, w_up.T)
    unused_two, norm_back_two = jax.vjp(normed, middle, gain_two_f)
    grad_middle, grad_gain_two = norm_back_two(grad_normal_two)
    grad_middle = grad_middle + grad_rows.astype(jnp.float32)
    ffn_terms = (
        lax.psum_scatter(
            grad_gain_two.astype(jnp.bfloat16), "dp", scatter_dimension=0, tiled=True
        ).astype(jnp.float32),
        lax.psum_scatter(
            grad_wgate.astype(jnp.bfloat16), "dp", scatter_dimension=0, tiled=True
        ).astype(jnp.float32),
        lax.psum_scatter(
            grad_wup.astype(jnp.bfloat16), "dp", scatter_dimension=0, tiled=True
        ).astype(jnp.float32),
        lax.psum_scatter(
            grad_down.astype(jnp.bfloat16), "dp", scatter_dimension=0, tiled=True
        ).astype(jnp.float32),
    )
    ffn_total = (
        lax.psum(ffn_terms[0].astype(jnp.bfloat16), "ctx").astype(jnp.float32),
        lax.psum(ffn_terms[1].astype(jnp.bfloat16), "ctx").astype(jnp.float32),
        lax.psum(ffn_terms[2].astype(jnp.bfloat16), "ctx").astype(jnp.float32),
        lax.psum(ffn_terms[3].astype(jnp.bfloat16), "ctx").astype(jnp.float32),
    )
    grad_branch = grad_middle.astype(jnp.bfloat16)
    grad_woutput = product(mixed_rows.T, grad_branch)
    grad_mixed = product(grad_branch, w_output.T).astype(jnp.bfloat16)
    grad_query, grad_keys_all, grad_values_all = lax.map(
        attend_back, (shaped(query), keys_all, values_all, shaped(grad_mixed), logsum)
    )
    grad_keys, grad_values = (
        lax.psum_scatter(
            grad_keys_all.astype(jnp.bfloat16), "ctx", scatter_dimension=1, tiled=True
        ).astype(jnp.float32),
        lax.psum_scatter(
            grad_values_all.astype(jnp.bfloat16), "ctx", scatter_dimension=1, tiled=True
        ).astype(jnp.float32),
    )
    grad_keys = grad_keys.astype(jnp.bfloat16)
    grad_values = grad_values.astype(jnp.bfloat16)
    grad_query = grad_query.reshape(rows, width)
    grad_keys = grad_keys.reshape(rows, width)
    grad_values = grad_values.reshape(rows, width)
    grad_wquery = product(normal_one.T, grad_query)
    grad_wkey = product(normal_one.T, grad_keys)
    grad_wvalue = product(normal_one.T, grad_values)
    grad_normal_one = (
        product(grad_query, w_query.T)
        + product(grad_keys, w_key.T)
        + product(grad_values, w_value.T)
    )
    unused_one, norm_back_one = jax.vjp(normed, inputs, gain_one_f)
    grad_inputs, grad_gain_one = norm_back_one(grad_normal_one)
    in_grad = (grad_inputs + grad_middle).astype(jnp.bfloat16).reshape(seqs, local, width)
    attn_terms = (
        lax.psum_scatter(
            grad_gain_one.astype(jnp.bfloat16), "dp", scatter_dimension=0, tiled=True
        ).astype(jnp.float32),
        lax.psum_scatter(
            grad_wquery.astype(jnp.bfloat16), "dp", scatter_dimension=0, tiled=True
        ).astype(jnp.float32),
        lax.psum_scatter(
            grad_wkey.astype(jnp.bfloat16), "dp", scatter_dimension=0, tiled=True
        ).astype(jnp.float32),
        lax.psum_scatter(
            grad_wvalue.astype(jnp.bfloat16), "dp", scatter_dimension=0, tiled=True
        ).astype(jnp.float32),
        lax.psum_scatter(
            grad_woutput.astype(jnp.bfloat16), "dp", scatter_dimension=0, tiled=True
        ).astype(jnp.float32),
    )
    attn_total = (
        lax.psum(attn_terms[0].astype(jnp.bfloat16), "ctx").astype(jnp.float32),
        lax.psum(attn_terms[1].astype(jnp.bfloat16), "ctx").astype(jnp.float32),
        lax.psum(attn_terms[2].astype(jnp.bfloat16), "ctx").astype(jnp.float32),
        lax.psum(attn_terms[3].astype(jnp.bfloat16), "ctx").astype(jnp.float32),
        lax.psum(attn_terms[4].astype(jnp.bfloat16), "ctx").astype(jnp.float32),
    )
    return (
        layer_out,
        in_grad,
        attn_total[0],
        attn_total[1],
        attn_total[2],
        attn_total[3],
        attn_total[4],
        ffn_total[0],
        ffn_total[1],
        ffn_total[2],
        ffn_total[3],
    )


def solution(mesh):
    in_specs = (
        P("dp", "ctx", None),
        P("dp", "ctx", None),
        P("dp"),
        P("dp", None),
        P("dp", None),
        P("dp", None),
        P("dp", None),
        P("dp"),
        P("dp", None),
        P("dp", None),
        P("dp", None),
    )
    out_specs = (
        P("dp", "ctx", None),
        P("dp", "ctx", None),
        P("dp"),
        P("dp", None),
        P("dp", None),
        P("dp", None),
        P("dp", None),
        P("dp"),
        P("dp", None),
        P("dp", None),
        P("dp", None),
    )
    return jax.shard_map(
        on_device, mesh=mesh, in_specs=in_specs, out_specs=out_specs, check_vma=False
    )
```

profile of v0, /device:TPU:0, one launch (start us, length us, event | category | flops | bytes accessed | tf_op | source)
XLA Modules:
  0.0 1048.5 jit_solution(17920821551046934564)
XLA Ops:
  13.8 7.7 all-gather.18.cloned.1.call-done
  24.3 9.2 all-gather.14.cloned.1.call-done
  40.8 4.7 all-gather.16.cloned.1.call-done
  47.5 96.6 %all-gather.30.cloned.1.call-done = bf16[4096,768]{1,0:T(8,128)(2,1)} async-done(((bf16[256,768]{1,0:T(8,128)(2,1)}), bf16[4096,768]{1,0:T(8,128)(2,1)}) %all-gather.30.cloned.1.call-update) | async-done | bytes 6291472 | tf_op jit(solution)/shard_map/all_gather | solution.py:117
  144.0 8.7 copy.36
  152.7 22.9 %multiply_reduce_fusion.1 = (f32[12,256]{1,0:T(8,128)S(1)}, f32[12,256,4096]{2,1,0:T(8,128)}) fusion(bf16[256,12,64]{0,2,1:T(8,128)(2,1)S(1)} %bitcast.127, bf16[4096,12,64]{0,2,1:T(8,128)(2,1)} %bitcast.119), kind=kOutput, calls=%fused_computation.6 | convolution fusion | flops 1635775488 | bytes 57028608 | tf_op jit(solution)/shard_map/while/body/eval_jaxpr/qhd,khd->hqk/dot_general | solution.py:26
  175.7 20.5 %fusion = f32[12,256]{1,0:T(8,128)S(1)} fusion(f32[12,256,4096]{2,1,0:T(8,128)} %get-tuple-element.75, f32[12,256]{1,0:T(8,128)S(1)} %get-tuple-element.74), kind=kLoop, calls=%fused_computation.5 | loop fusion | flops 37745664 | bytes 50356224 | tf_op jit(solution)/shard_map/while/body/eval_jaxpr/reduce_sum | solution.py:36
  196.2 43.5 %all-gather.28.cloned.1.call-done = bf16[4096,768]{1,0:T(8,128)(2,1)} async-done(((bf16[256,768]{1,0:T(8,128)(2,1)}), bf16[4096,768]{1,0:T(8,128)(2,1)}) %all-gather.28.cloned.1.call-update) | async-done | bytes 6291472 | tf_op jit(solution)/shard_map/all_gather | solution.py:118
  239.7 8.7 copy.34
  248.4 22.0 %fusion.19 = bf16[12,64,256]{2,1,0:T(8,128)(2,1)S(1)} fusion(bf16[4096,12,64]{0,2,1:T(8,128)(2,1)} %bitcast.121, f32[12,256,4096]{2,1,0:T(8,128)} %get-tuple-element.75, f32[12,256]{1,0:T(8,128)S(1)} %fusion, f32[12,256]{1,0:T(8,128)S(1)} %get-tuple-element.74), kind=kOutput, calls=%fused_computation.45 | convolution fusion | flops 1661140992 | bytes 57040896 | tf_op jit(solution)/shard_map/while/body/eval_jaxpr/hqk,khd->qhd/dot_general | solution.py:38
  272.6 4.6 fusion.57
  278.5 4.2 fusion.58
  282.7 10.7 %all-gather.26.cloned.1.call-done = bf16[2048,768]{1,0:T(8,128)(2,1)} async-done(((bf16[1024,768]{1,0:T(8,128)(2,1)}), bf16[2048,768]{1,0:T(8,128)(2,1)}) %all-gather.26.cloned.1.call-update) | async-done | bytes 3145744 | tf_op jit(solution)/shard_map/all_gather | solution.py:127
  293.3 6.7 multiply_convert_fusion.2
  305.3 35.5 %multiply_reduce_fusion = (f32[12,256]{1,0:T(8,128)}, f32[12,256,4096]{2,1,0:T(8,128)}) fusion(f32[12,256,4096]{2,1,0:T(8,128)} %get-tuple-element.75, f32[12,256]{1,0:T(8,128)S(1)} %log_add_fusion, bf16[256,12,64]{0,2,1:T(8,128)(2,1)S(1)} %bitcast.125, bf16[4096,12,64]{0,2,1:T(8,128)(2,1)} %bitcast.122), kind=kOutput, calls=%fused_computation.1 | convolution fusion | flops 1660941312 | bytes 107372544 | tf_op jit(solution)/shard_map/while/body/eval_jaxpr/qhd,khd->hqk/dot_general | solution.py:45
  340.8 40.2 %multiply_convert_fusion = bf16[12,256,4096]{2,1,0:T(8,128)(2,1)} fusion(f32[12,256,4096]{2,1,0:T(8,128)} %get-tuple-element.80, f32[12,256,4096]{2,1,0:T(8,128)} %get-tuple-element.75, f32[12,256]{1,0:T(8,128)} %get-tuple-element.79, f32[12,256]{1,0:T(8,128)S(1)} %log_add_fusion), kind=kLoop, calls=%fused_computation | loop fusion | flops 62914560 | bytes 125853696 | tf_op jit(solution)/shard_map/while/body/eval_jaxpr/convert_element_type | solution.py:49
  381.0 15.2 %multiply_convert_fusion.1 = bf16[12,64,4096]{2,1,0:T(8,128)(2,1)} fusion(bf16[256,12,64]{0,2,1:T(8,128)(2,1)S(1)} %bitcast.128, bf16[12,256,4096]{2,1,0:T(8,128)(2,1)} %multiply_convert_fusion), kind=kOutput, calls=%fused_computation.12 | convolution fusion | flops 1616904192 | bytes 31850496 | tf_op jit(solution)/shard_map/while/body/eval_jaxpr/hqk,qhd->khd/dot_general | solution.py:64
  396.3 22.0 %fusion.7 = bf16[12,64,4096]{2,1,0:T(8,128)(2,1)} fusion(bf16[256,12,64]{0,2,1:T(8,128)(2,1)S(1)} %bitcast.126, f32[12,256,4096]{2,1,0:T(8,128)} %get-tuple-element.75, f32[12,256]{1,0:T(8,128)S(1)} %log_add_fusion), kind=kOutput, calls=%fused_computation.13 | convolution fusion | flops 1651507200 | bytes 57028608 | tf_op jit(solution)/shard_map/while/body/eval_jaxpr/hqk,qhd->khd/dot_general | solution.py:67
  418.4 14.4 %fusion.18 = bf16[12,64,256]{2,1,0:T(8,128)(2,1)S(1)} fusion(bf16[4096,12,64]{0,2,1:T(8,128)(2,1)} %bitcast.120, bf16[12,256,4096]{2,1,0:T(8,128)(2,1)} %multiply_convert_fusion), kind=kOutput, calls=%fused_computation.44 | convolution fusion | flops 1611005952 | bytes 31850496 | tf_op jit(solution)/shard_map/while/body/eval_jaxpr/hqk,khd->qhd/dot_general | solution.py:54
  436.2 3.9 convolution_convert_fusion.2
  448.1 95.9 %reduce-scatter.10.cloned.1.call-done = bf16[1,256,768]{1,2,0:T(8,128)(2,1)} async-done(((bf16[1,4096,768]{1,2,0:T(8,128)(2,1)}), bf16[1,256,768]{1,2,0:T(8,128)(2,1)}) %reduce-scatter.10.cloned.1.call-update) | async-done | bytes 393232 | tf_op jit(solution)/shard_map/reduce_scatter | solution.py:191
  546.7 147.8 %reduce-scatter.12.cloned.1.call-done = bf16[1,256,768]{1,2,0:T(8,128)(2,1)} async-done(((bf16[1,4096,768]{1,2,0:T(8,128)(2,1)}), bf16[1,256,768]{1,2,0:T(8,128)(2,1)}) %reduce-scatter.12.cloned.1.call-update) | async-done | bytes 393232 | tf_op jit(solution)/shard_map/reduce_scatter | solution.py:194
  697.4 7.5 reduce-scatter.14.cloned.1.call-done
  705.0 12.8 %reduce-scatter.20.cloned.1.call-done = bf16[384,768]{1,0:T(8,128)(2,1)} async-done(((bf16[768,768]{1,0:T(8,128)(2,1)}), bf16[384,768]{1,0:T(8,128)(2,1)}) %reduce-scatter.20.cloned.1.call-update) | async-done | bytes 589840 | tf_op jit(solution)/shard_map/reduce_scatter | solution.py:227
  717.7 14.8 %reduce-scatter.22.cloned.1.call-done = bf16[384,2048]{1,0:T(8,128)(2,1)} async-done(((bf16[768,2048]{1,0:T(8,128)(2,1)}), bf16[384,2048]{1,0:T(8,128)(2,1)}) %reduce-scatter.22.cloned.1.call-update) | async-done | bytes 1572880 | tf_op jit(solution)/shard_map/reduce_scatter | solution.py:168
  732.6 14.9 %reduce-scatter.24.cloned.1.call-done = bf16[384,2048]{1,0:T(8,128)(2,1)} async-done(((bf16[768,2048]{1,0:T(8,128)(2,1)}), bf16[384,2048]{1,0:T(8,128)(2,1)}) %reduce-scatter.24.cloned.1.call-update) | async-done | bytes 1572880 | tf_op jit(solution)/shard_map/reduce_scatter | solution.py:171
  747.4 14.8 %reduce-scatter.26.cloned.1.call-done = bf16[1024,768]{1,0:T(8,128)(2,1)} async-done(((bf16[2048,768]{1,0:T(8,128)(2,1)}), bf16[1024,768]{1,0:T(8,128)(2,1)}) %reduce-scatter.26.cloned.1.call-update) | async-done | bytes 1572880 | tf_op jit(solution)/shard_map/reduce_scatter | solution.py:174
  762.2 12.6 %reduce-scatter.16.cloned.1.call-done = bf16[384,768]{1,0:T(8,128)(2,1)} async-done(((bf16[768,768]{1,0:T(8,128)(2,1)}), bf16[384,768]{1,0:T(8,128)(2,1)}) %reduce-scatter.16.cloned.1.call-update) | async-done | bytes 589840 | tf_op jit(solution)/shard_map/reduce_scatter | solution.py:221
  774.8 12.6 %reduce-scatter.18.cloned.1.call-done = bf16[384,768]{1,0:T(8,128)(2,1)} async-done(((bf16[768,768]{1,0:T(8,128)(2,1)}), bf16[384,768]{1,0:T(8,128)(2,1)}) %reduce-scatter.18.cloned.1.call-update) | async-done | bytes 589840 | tf_op jit(solution)/shard_map/reduce_scatter | solution.py:224
  791.1 3.8 fusion.20
  798.8 43.9 %all-reduce.2 = (bf16[384]{0:T(512)(128)(2,1)S(1)}, bf16[384]{0:T(512)(128)(2,1)S(1)}) all-reduce(bf16[384]{0:T(512)(128)(2,1)S(1)} %dynamic-slice.3, bf16[384]{0:T(512)(128)(2,1)S(1)} %dynamic-slice.5), channel_id=1, replica_groups=mesh['dp'=2,'ctx'=16] {'ctx'}, use_global_device_ids=true, to_apply=%region_11.12 | all-reduce | flops 768 | bytes 3072 | tf_op jit(solution)/shard_map/psum | solution.py:232
  844.9 184.0 %all-reduce.7.cloned.1.call-done = (bf16[384,768]{1,0:T(8,128)(2,1)}, bf16[384,768]{1,0:T(8,128)(2,1)}, bf16[384,768]{1,0:T(8,128)(2,1)}, bf16[384,768]{1,0:T(8,...) async-done(((bf16[384,768]{1,0:T(8,128)(2,1)}, bf16[384,768]{1,0:T(8,128)(2,1)}, bf16[384,768]{1,0:T(8,128)(2,1)}, ...) | async-done | bytes 7077904 | tf_op jit(solution)/shard_map/psum | solution.py:233
  (153 shorter events, 65.7 us)
Async XLA Ops:
  7.2 26.3 %copy-start = (bf16[1,256,768]{2,1,0:T(8,128)(2,1)S(1)}, bf16[1,256,768]{2,1,0:T(8,128)(2,1)}, u32[]{:S(2)}) copy-start(bf16[1,256,768]{2,1,0:T(8,128)(2,1)} %param.11) | copy-start | bytes 1179652
  7.2 14.3 %all-gather.18.cloned.1.call-start = ((), (), s32[]{:S(2)}) async-start(), calls=%async_computation.11 | async-start | bytes 1769472 | tf_op jit(solution)/shard_map/all_gather | solution.py:106
  7.9 25.6 %all-gather.14.cloned.1.call-start = ((), (), s32[]{:S(2)}) async-start(), calls=%async_computation.9 | async-start | bytes 1769472 | tf_op jit(solution)/shard_map/all_gather | solution.py:107
  8.7 36.8 %all-gather.16.cloned.1.call-start = ((), (), s32[]{:S(2)}) async-start(), calls=%async_computation.10 | async-start | bytes 1769472 | tf_op jit(solution)/shard_map/all_gather | solution.py:105
  9.4 134.6 %all-gather.30.cloned.1.call-start = ((), (), s32[]{:S(2)}) async-start(), calls=%async_computation.26 | async-start | bytes 6684672 | tf_op jit(solution)/shard_map/all_gather | solution.py:117
  12.1 33.4 %copy-start.23 = (f32[768]{0:T(1024)}, f32[768]{0:T(1024)S(1)}, u32[]{:S(2)}) copy-start(f32[768]{0:T(1024)S(1)} %reshape.240) | copy-start | bytes 9220
  13.8 31.6 %copy-start.25 = (f32[256]{0:T(256)}, f32[256]{0:T(256)S(1)}, u32[]{:S(2)}) copy-start(f32[256]{0:T(256)S(1)} %fusion.47) | copy-start | bytes 3076
  24.2 215.5 %all-gather.28.cloned.1.call-start = ((), (), s32[]{:S(2)}) async-start(), calls=%async_computation.25 | async-start | bytes 6684672 | tf_op jit(solution)/shard_map/all_gather | solution.py:118
  36.1 234.4 %all-gather.20.cloned.1.call-start = ((), (), s32[]{:S(2)}) async-start(), calls=%async_computation.12 | async-start | bytes 1769472 | tf_op jit(solution)/shard_map/all_gather | solution.py:108
  36.6 235.9 %all-gather.22.cloned.1.call-start = ((), (), s32[]{:S(2)}) async-start(), calls=%async_computation.13 | async-start | bytes 4718592 | tf_op jit(solution)/shard_map/all_gather | solution.py:125
  37.4 241.1 %all-gather.24.cloned.1.call-start = ((), (), s32[]{:S(2)}) async-start(), calls=%async_computation.14 | async-start | bytes 4718592 | tf_op jit(solution)/shard_map/all_gather | solution.py:126
  38.1 255.2 %all-gather.26.cloned.1.call-start = ((), (), s32[]{:S(2)}) async-start(), calls=%async_computation.15 | async-start | bytes 4718592 | tf_op jit(solution)/shard_map/all_gather | solution.py:127
  38.9 505.1 %reduce-scatter.10.cloned.1.call-start = ((), (), s32[]{:S(2)}) async-start(), calls=%async_computation.16 | async-start | bytes 6684672 | tf_op jit(solution)/shard_map/reduce_scatter | solution.py:191
  47.4 105.3 %copy-start.3 = (bf16[256,768]{0,1:T(8,128)(2,1)}, bf16[256,768]{0,1:T(8,128)(2,1)S(1)}, u32[]{:S(2)}) copy-start(bf16[256,768]{0,1:T(8,128)(2,1)S(1)} %copy.35) | copy-start | bytes 1179652
  277.2 16.1 %copy-start.11 = (bf16[1,256,768]{2,1,0:T(8,128)(2,1)S(1)}, bf16[1,256,768]{2,1,0:T(8,128)(2,1)}, u32[]{:S(2)}) copy-start(bf16[1,256,768]{2,1,0:T(8,128)(2,1)} %param.12) | copy-start | bytes 1179652
  293.3 6.7 copy-start.10
  340.8 40.2 %copy-start.4 = (bf16[256,768]{0,1:T(8,128)(2,1)S(1)}, bf16[256,768]{0,1:T(8,128)(2,1)}, u32[]{:S(2)}) copy-start(bf16[256,768]{0,1:T(8,128)(2,1)} %copy-done.3) | copy-start | bytes 1179652
  396.3 298.2 %reduce-scatter.12.cloned.1.call-start = ((), (), s32[]{:S(2)}) async-start(), calls=%async_computation.17 | async-start | bytes 6684672 | tf_op jit(solution)/shard_map/reduce_scatter | solution.py:194
  418.3 14.5 %copy-start.24 = (f32[768]{0:T(1024)S(1)}, f32[768]{0:T(1024)}, u32[]{:S(2)}) copy-start(f32[768]{0:T(1024)} %copy-done.23) | copy-start | bytes 9220
  418.4 14.5 %copy-start.26 = (f32[256]{0:T(256)S(1)}, f32[256]{0:T(256)}, u32[]{:S(2)}) copy-start(f32[256]{0:T(256)} %copy-done.25) | copy-start | bytes 3076
  418.4 286.6 %reduce-scatter.14.cloned.1.call-start = ((), (), s32[]{:S(2)}) async-start(), calls=%async_computation.18 | async-start | bytes 1769472 | tf_op jit(solution)/shard_map/reduce_scatter | solution.py:218
  434.5 283.2 %reduce-scatter.20.cloned.1.call-start = ((), (), s32[]{:S(2)}) async-start(), calls=%async_computation.21 | async-start | bytes 1769472 | tf_op jit(solution)/shard_map/reduce_scatter | solution.py:227
  436.1 296.4 %reduce-scatter.22.cloned.1.call-start = ((), (), s32[]{:S(2)}) async-start(), calls=%async_computation.22 | async-start | bytes 4718592 | tf_op jit(solution)/shard_map/reduce_scatter | solution.py:168
  440.1 307.3 %reduce-scatter.24.cloned.1.call-start = ((), (), s32[]{:S(2)}) async-start(), calls=%async_computation.23 | async-start | bytes 4718592 | tf_op jit(solution)/shard_map/reduce_scatter | solution.py:171
  444.0 318.1 %reduce-scatter.26.cloned.1.call-start = ((), (), s32[]{:S(2)}) async-start(), calls=%async_computation.24 | async-start | bytes 4718592 | tf_op jit(solution)/shard_map/reduce_scatter | solution.py:174
  448.1 326.7 %reduce-scatter.16.cloned.1.call-start = ((), (), s32[]{:S(2)}) async-start(), calls=%async_computation.19 | async-start | bytes 1769472 | tf_op jit(solution)/shard_map/reduce_scatter | solution.py:221
  546.6 240.7 %reduce-scatter.18.cloned.1.call-start = ((), (), s32[]{:S(2)}) async-start(), calls=%async_computation.20 | async-start | bytes 1769472 | tf_op jit(solution)/shard_map/reduce_scatter | solution.py:224
  697.1 331.8 %all-reduce.7.cloned.1.call-start = ((), (), s32[]{:S(2)}) async-start(), calls=%async_computation.27 | async-start | bytes 14155776 | tf_op jit(solution)/shard_map/psum | solution.py:233
  794.9 49.0 %copy-start.28 = (f32[256]{0:T(256)S(1)}, f32[256]{0:T(256)}, u32[]{:S(2)}) copy-start(f32[256]{0:T(256)} %copy-done.27) | copy-start | bytes 3076
  1028.9 4.5 copy-start.22
  1028.9 5.6 copy-start.21
  1028.9 6.7 copy-start.17
  (19 other events, 49.3 us)
Sparse Core Ops, SparseCore 0:
  9.6 11.9 all-gather.17
  23.1 10.3 all-gather.13
  35.0 10.3 all-gather.15
  48.7 95.2 all-gather.29
  147.2 92.4 all-gather.27
  241.1 7.4 all-gather.19
  250.2 13.2 all-gather.21
  265.0 13.3 all-gather.23
  280.0 13.2 all-gather.25
  396.4 147.5 reduce-scatter.9
  549.2 145.1 reduce-scatter.11
  697.1 7.7 reduce-scatter.13
  707.9 9.8 reduce-scatter.19
  720.4 12.0 reduce-scatter.21
  735.3 12.0 reduce-scatter.23
  750.1 12.0 reduce-scatter.25
  764.9 9.8 reduce-scatter.15
  777.5 9.8 reduce-scatter.17
  794.9 233.9 all-reduce.6
where the time goes:
time: 1060 us; the launch traced here: 1050 us
  waiting for transfers between devices  696 us (66%)
  matrix products  184 us (17%)
  other arithmetic  77.1 us (7%)
  blocking collectives  50.1 us (5%)
  local copies, waits for them, and re-layouts  24.6 us (2%)
  between operations  15.5 us (1%)
    psum x1, waiting for transfers between devices, on_device(): lax.psum(attn_terms[1].astype(jnp.bfloat16), 'ctx').astype(jnp.float32)  184 us
    reduce_scatter x1, waiting for transfers between devices, on_device(): lax.psum_scatter(grad_values_all.astype(jnp.bfloat16), 'ctx', scatter_dim...  148 us
    all_gather x1, waiting for transfers between devices, on_device(): lax.all_gather(shaped(keys), 'ctx', axis=1, tiled=True)  96.6 us
    reduce_scatter x1, waiting for transfers between devices, on_device(): lax.psum_scatter(grad_keys_all.astype(jnp.bfloat16), 'ctx', scatter_dimen...  95.9 us
    dot_general x21, matrix products, product(): return jnp.dot(left, right, preferred_element_type=jnp.float32)  52 us
    psum x1, blocking collectives, on_device(): lax.psum(attn_terms[0].astype(jnp.bfloat16), 'ctx').astype(jnp.float32)  43.9 us
    all_gather x1, waiting for transfers between devices, on_device(): lax.all_gather(shaped(values), 'ctx', axis=1, tiled=True)  43.5 us
    convert_element_type x1, other arithmetic, back_core(): grad_score = (probs * (grad_prob - delta[..., None])).astype(jnp.bfloat16)  40.2 us
  transfers between devices with their start and end apart: 19, of which 17 were waited for; matrix products, arithmetic and copies ran while one was open for 16% of the time, Pallas kernels for 0%

commit v1 on v0

v1 whole, which is shorter than its diff:
```python
import functools
import math

import jax
import jax.numpy as jnp
from jax import lax
from jax.experimental import pallas as pl
from jax.experimental.pallas import tpu as pltpu
from jax.sharding import PartitionSpec as P

HEADS = 12
HEAD_DIM = 64
EPS = 1e-06
LOG2E = 1.4426950408889634
SCALE = HEAD_DIM ** (-0.5)
AXES = ("dp", "ctx")
F32 = jnp.float32
BF16 = jnp.bfloat16


def dotg(a, b, ca, cb):
    return lax.dot_general(a, b, (((ca,), (cb,)), ((), ())), preferred_element_type=F32)


def attend_kernel(heads, key_block, q_ref, *refs):
    sources = refs[:-3]
    o_ref, low_ref, lse_ref = refs[-3:]
    tokens = q_ref.shape[1]
    width = heads * HEAD_DIM
    for h in range(heads):
        hs = slice(h * HEAD_DIM, (h + 1) * HEAD_DIM)
        vs = slice(width + h * HEAD_DIM, width + (h + 1) * HEAD_DIM)
        query = q_ref[hs, :] * BF16(SCALE)
        top = jnp.full((1, tokens), -jnp.inf, F32)
        total = jnp.zeros((1, tokens), F32)
        acc = jnp.zeros((HEAD_DIM, tokens), F32)
        for source in sources:
            for at in range(0, source.shape[1], key_block):
                ks = slice(at, at + key_block)
                scores = dotg(source[hs, ks], query, 0, 0) * LOG2E
                new_top = jnp.maximum(top, jnp.max(scores, axis=0, keepdims=True))
                decay = jnp.exp2(top - new_top)
                probs = jnp.exp2(scores - new_top)
                total = total * decay + jnp.sum(probs, axis=0, keepdims=True)
                acc = acc * decay + jnp.dot(
                    source[vs, ks], probs.astype(BF16), preferred_element_type=F32
                )
                top = new_top
        out = acc / total
        o_ref[hs, :] = out
        low_ref[hs, :] = out.astype(BF16)
        lse_ref[h : h + 1, :] = top + jnp.log2(total)


def attend(query, sources, key_block=1024):
    width, tokens = query.shape
    heads = width // HEAD_DIM
    return pl.pallas_call(
        functools.partial(attend_kernel, heads, key_block),
        out_shape=(
            jax.ShapeDtypeStruct((width, tokens), F32),
            jax.ShapeDtypeStruct((width, tokens), BF16),
            jax.ShapeDtypeStruct((heads, tokens), F32),
        ),
        compiler_params=pltpu.CompilerParams(vmem_limit_bytes=60 << 20),
        name="attend",
    )(query, *sources)


def attend_back_kernel(heads, key_block, q_ref, do_ref, o_ref, lse_ref, *refs):
    n = (len(refs) - 1) // 2
    sources, dq_ref, outs = refs[:n], refs[n], refs[n + 1 :]
    width = heads * HEAD_DIM
    for h in range(heads):
        hs = slice(h * HEAD_DIM, (h + 1) * HEAD_DIM)
        vs = slice(width + h * HEAD_DIM, width + (h + 1) * HEAD_DIM)
        query = q_ref[hs, :] * BF16(SCALE)
        grad = do_ref[hs, :]
        lse = lse_ref[h : h + 1, :]
        delta = jnp.sum(grad.astype(F32) * o_ref[hs, :], axis=0, keepdims=True)
        dq = jnp.zeros(query.shape, F32)
        for source, out in zip(sources, outs):
            for at in range(0, source.shape[1], key_block):
                ks = slice(at, at + key_block)
                keys, values = source[hs, ks], source[vs, ks]
                probs = jnp.exp2(dotg(keys, query, 0, 0) * LOG2E - lse)
                gap = dotg(values, grad, 0, 0) - delta
                low = probs.astype(BF16)
                ds = (probs * gap).astype(BF16)
                out[vs, ks] = dotg(grad, low, 1, 1).astype(BF16)
                out[hs, ks] = dotg(query, ds, 1, 1).astype(BF16)
                dq = dq + jnp.dot(keys, ds, preferred_element_type=F32)
        dq_ref[hs, :] = (dq * SCALE).astype(BF16)


def attend_back(query, grad, out, lse, sources, key_block=256):
    heads = query.shape[0] // HEAD_DIM
    outs = pl.pallas_call(
        functools.partial(attend_back_kernel, heads, key_block),
        out_shape=(jax.ShapeDtypeStruct(query.shape, BF16),)
        + tuple(jax.ShapeDtypeStruct(s.shape, BF16) for s in sources),
        compiler_params=pltpu.CompilerParams(vmem_limit_bytes=60 << 20),
        name="attend_back",
    )(query, grad, out, lse, *sources)
    return outs[0], list(outs[1:])


class Plan:
    def __init__(self, dp, ctx):
        self.dp, self.ctx = dp, ctx
        self.groups = math.gcd(HEADS, ctx)
        self.rest = ctx // self.groups
        self.bits = self.rest.bit_length() - 1
        assert 1 << self.bits == self.rest and self.groups & (self.groups - 1) == 0

    def bit(self, parity, step):
        return step if parity == 0 else self.bits - 1 - step

    def rest_perm(self, step):
        return [
            (d * self.ctx + c, d * self.ctx + (c ^ (1 << self.bit(d % 2, step))))
            for d in range(self.dp)
            for c in range(self.ctx)
        ]

    def group_perm(self, s):
        return [(c, c ^ (s * self.rest)) for c in range(self.ctx)]

    def group(self):
        return lax.axis_index("ctx") // self.rest

    def my_bit(self, step):
        c = lax.axis_index("ctx")
        even = (c >> self.bit(0, step)) & 1
        odd = (c >> self.bit(1, step)) & 1
        return jnp.where(lax.axis_index("dp") % 2 == 0, even, odd)

    def over_rest(self, value, step):
        return lax.ppermute(value, AXES, self.rest_perm(step))

    def over_group(self, value, s):
        return value if s == 0 else lax.ppermute(value, "ctx", self.group_perm(s))

    def gather_rest(self, value):
        blocks = [value]
        for step in range(self.bits):
            blocks = blocks + [self.over_rest(b, step) for b in blocks]
        return blocks

    def scatter_rest(self, blocks):
        for step in reversed(range(self.bits)):
            half = len(blocks) // 2
            came = [self.over_rest(b, step) for b in blocks[half:]]
            blocks = [add_low(a, b) for a, b in zip(blocks[:half], came)]
        return blocks[0]

    def to_heads(self, value):
        size = value.shape[0] // self.groups
        return [
            self.over_group(
                lax.dynamic_slice_in_dim(value, (self.group() ^ s) * size, size, 0), s
            )
            for s in range(self.groups)
        ]

    def to_tokens(self, pieces):
        came = [self.over_group(p, s) for s, p in enumerate(pieces)]
        return self.natural(came)

    def natural(self, pieces):
        g = self.group()
        step = 1
        while step < self.groups:
            odd = (g & step) != 0
            pieces = [
                jnp.where(odd, pieces[i ^ step], pieces[i]) for i in range(self.groups)
            ]
            step *= 2
        return jnp.concatenate(pieces, axis=0)

    def sum_ctx(self, value):
        for step in range(self.bits):
            half = value.shape[0] // 2
            b = self.my_bit(step)
            kept = lax.dynamic_slice_in_dim(value, b * half, half, 0)
            gone = lax.dynamic_slice_in_dim(value, (1 - b) * half, half, 0)
            value = add_low(kept, self.over_rest(gone, step))
        pieces = self.to_heads(value)
        value = functools.reduce(jnp.add, [p.astype(F32) for p in pieces]).astype(BF16)
        value = self.natural(
            [self.over_group(value, s) for s in range(self.groups)]
        )
        for step in reversed(range(self.bits)):
            b = self.my_bit(step)
            came = self.over_rest(value, step)
            value = jnp.where(
                b == 0,
                jnp.concatenate([value, came], axis=0),
                jnp.concatenate([came, value], axis=0),
            )
        return value.astype(F32)

    def sum_small(self, value):
        for step in range(self.bits):
            value = value + self.over_rest(value, step)
        return functools.reduce(
            jnp.add, [self.over_group(value, s) for s in range(self.groups)]
        )


def add_low(a, b):
    return (a.astype(F32) + b.astype(F32)).astype(BF16)


class Pair:
    def __init__(self, dp):
        self.dp = dp
        self.me = lax.axis_index("dp")

    def swap(self, value):
        return lax.ppermute(value, "dp", [(0, 1), (1, 0)])

    def gather(self, weight):
        if self.dp == 2:
            return [weight, self.swap(weight)]
        return [lax.all_gather(weight, "dp", axis=0, tiled=True)]

    def part(self, value, i, axis):
        if self.dp != 2:
            return value
        half = value.shape[axis] // 2
        at = jnp.where(self.me == i, 0, half)
        return lax.dynamic_slice_in_dim(value, at, half, axis)

    def join(self, parts, axis):
        if len(parts) == 1:
            return parts[0]
        return jnp.where(
            self.me == 0,
            jnp.concatenate(parts, axis),
            jnp.concatenate(parts[::-1], axis),
        )

    def times(self, value, axis, weight, contract):
        return functools.reduce(
            jnp.add,
            [
                contract(self.part(value, i, axis), w)
                for i, w in enumerate(weight)
            ],
        )

    def grad(self, left, row_axis, right, right_axis):
        token_axis = 1 - row_axis
        if self.dp != 2:
            return lax.psum_scatter(
                dotg(left, right, token_axis, right_axis).astype(BF16),
                "dp",
                scatter_dimension=0,
                tiled=True,
            )
        own, other = self.part(left, 0, row_axis), self.part(left, 1, row_axis)
        lefts = jnp.concatenate([own, self.swap(other)], token_axis)
        rights = jnp.concatenate([right, self.swap(right)], right_axis)
        return dotg(lefts, rights, token_axis, right_axis).astype(BF16)

    def gain(self, part):
        if self.dp != 2:
            return lax.psum_scatter(part, "dp", scatter_dimension=0, tiled=True)
        return self.part(part, 0, 0) + self.swap(self.part(part, 1, 0))


def scaled(rows):
    return lax.rsqrt(jnp.mean(rows * rows, axis=-1, keepdims=True) + EPS)


def gated(gate, upper):
    return jax.nn.gelu(gate, approximate=True) * upper


def norm_back(rows, r, gain, grad):
    lead = gain * grad
    back = r * (lead - rows * (r * r) * jnp.mean(lead * rows, axis=-1, keepdims=True))
    return back, jnp.sum(grad * rows * r, axis=0)


def on_device(
    dp,
    ctx,
    layer_in,
    out_grad,
    first_gain,
    query_weight,
    key_weight,
    value_weight,
    output_weight,
    second_gain,
    gate_weight,
    up_weight,
    down_weight,
):
    plan, pair = Plan(dp, ctx), Pair(dp)
    _, local, width = layer_in.shape
    group_width = width // plan.groups

    gain_one = pair.join(pair.gather(first_gain), 0).astype(F32)
    w_query, w_key, w_value = (
        pair.gather(w) for w in (query_weight, key_weight, value_weight)
    )
    x = layer_in.reshape(local, width).astype(F32)
    r1 = scaled(x)
    h1 = (x * r1 * gain_one).astype(BF16)

    def project(w):
        return pair.times(h1, 1, w, lambda a, b: dotg(b, a, 0, 1)).astype(BF16)

    keys, values, query = project(w_key), project(w_value), project(w_query)
    kv_pieces = [
        jnp.concatenate(p, axis=0) for p in zip(plan.to_heads(keys), plan.to_heads(values))
    ]
    kv = jnp.concatenate(kv_pieces, axis=1)
    q = jnp.concatenate(plan.to_heads(query), axis=1)
    sources = plan.gather_rest(kv)
    o_wide, o_low, lse = attend(q, sources)

    def by_token(value):
        return [value[:, i * local : (i + 1) * local] for i in range(plan.groups)]

    mixed = plan.to_tokens(by_token(o_low))

    w_output = pair.gather(output_weight)
    gain_two = pair.join(pair.gather(second_gain), 0).astype(F32)
    w_gate, w_up, w_down = (pair.gather(w) for w in (gate_weight, up_weight, down_weight))
    y1 = x + pair.times(mixed, 0, w_output, lambda a, b: dotg(a, b, 0, 0))
    r2 = scaled(y1)
    h2 = (y1 * r2 * gain_two).astype(BF16)
    gate = pair.times(h2, 1, w_gate, lambda a, b: dotg(a, b, 1, 0))
    upper = pair.times(h2, 1, w_up, lambda a, b: dotg(a, b, 1, 0))
    hidden = gated(gate, upper).astype(BF16)
    result = y1 + pair.times(hidden, 1, w_down, lambda a, b: dotg(a, b, 1, 0))
    layer_out = result.astype(BF16).reshape(layer_in.shape)

    dy = out_grad.reshape(local, width)
    down_term = pair.grad(hidden, 1, dy, 0)
    grad_hidden = pair.join([dotg(dy, w, 1, 1) for w in w_down], 1)
    _, gate_back = jax.vjp(gated, gate, upper)
    d_gate, d_up = gate_back(grad_hidden)
    d_gate, d_up = d_gate.astype(BF16), d_up.astype(BF16)
    gate_term = pair.grad(h2, 1, d_gate, 0)
    up_term = pair.grad(h2, 1, d_up, 0)
    dh2 = pair.join(
        [dotg(d_gate, a, 1, 1) + dotg(d_up, b, 1, 1) for a, b in zip(w_gate, w_up)], 1
    )
    back_two, gain_two_part = norm_back(y1, r2, gain_two, dh2)
    dy1 = back_two + dy.astype(F32)
    da = dy1.astype(BF16)
    output_term = pair.grad(mixed, 0, da, 0)
    d_mixed = pair.join([dotg(w, da, 1, 1) for w in w_output], 0).astype(BF16)

    do = jnp.concatenate(plan.to_heads(d_mixed), axis=1)
    dq, dkv = attend_back(q, do, o_wide, lse, sources)
    dkv = plan.scatter_rest(dkv)
    d_query = plan.to_tokens(by_token(dq))
    d_key = plan.to_tokens(by_token(dkv[:group_width]))
    d_value = plan.to_tokens(by_token(dkv[group_width:]))
    query_term = pair.grad(h1, 1, d_query, 1)
    key_term = pair.grad(h1, 1, d_key, 1)
    value_term = pair.grad(h1, 1, d_value, 1)
    dh1 = pair.join(
        [
            dotg(d_query, a, 0, 1) + dotg(d_key, b, 0, 1) + dotg(d_value, c, 0, 1)
            for a, b, c in zip(w_query, w_key, w_value)
        ],
        1,
    )
    back_one, gain_one_part = norm_back(x, r1, gain_one, dh1)
    in_grad = (back_one + dy1).astype(BF16).reshape(layer_in.shape)

    gains = plan.sum_small(
        jnp.stack([pair.gain(gain_one_part), pair.gain(gain_two_part)])
    )
    return (
        layer_out,
        in_grad,
        gains[0],
        plan.sum_ctx(query_term),
        plan.sum_ctx(key_term),
        plan.sum_ctx(value_term),
        plan.sum_ctx(output_term),
        gains[1],
        plan.sum_ctx(gate_term),
        plan.sum_ctx(up_term),
        plan.sum_ctx(down_term),
    )


def solution(mesh):
    tokens, matrix, vector = P("dp", "ctx", None), P("dp", None), P("dp")
    weights = (vector, matrix, matrix, matrix, matrix, vector, matrix, matrix, matrix)
    return jax.shard_map(
        functools.partial(on_device, mesh.shape["dp"], mesh.shape["ctx"]),
        mesh=mesh,
        in_specs=(tokens, tokens) + weights,
        out_specs=(tokens, tokens) + weights,
        check_vma=False,
    )
```

time: 1060 us -> 465 us (0.44)
  waiting for transfers between devices: 696 us -> 155 us
  starting transfers between devices: 1.02 us -> 162 us
  matrix products: 184 us -> 44.1 us
  Pallas kernels: 0 us -> 53.7 us
  blocking collectives: 50.1 us -> 0 us
  other arithmetic: 77.1 us -> 27.1 us
  local copies, waits for them, and re-layouts: 24.6 us -> 10.8 us
  between operations: 15.5 us -> 3.03 us
    reduce_scatter x9 -> x0, waiting for transfers between devices: 334 us -> none  [the longest x1 148 us: on_device(): lax.psum_scatter(grad_values_all.astype(jnp.bfloat16), 'ctx', scatter_dim...]
    psum x1 -> x0, waiting for transfers between devices: 184 us -> none  [on_device(): lax.psum(attn_terms[1].astype(jnp.bfloat16), 'ctx').astype(jnp.float32)]
    all_gather x9 -> x0, waiting for transfers between devices: 174 us -> none  [the longest x1 96.6 us: on_device(): lax.all_gather(shaped(keys), 'ctx', axis=1, tiled=True)]
    ppermute x0 -> x127, starting transfers between devices: none -> 162 us  [the longest x69 108 us: over_group(): return value if s == 0 else lax.ppermute(value, 'ctx', self.group_perm(s))]
    ppermute x0 -> x127, waiting for transfers between devices: none -> 155 us  [the longest x36 83.6 us: over_rest(): return lax.ppermute(value, AXES, self.rest_perm(step))]
    dot_general x27 -> x35, matrix products: 184 us -> 44.1 us  [dotg(): lax.dot_general(a, b, (((ca,), (cb,)), ((), ())), preferred_element_type=...]
    pallas_call x0 -> x2, Pallas kernels: none -> 53.7 us  [the longest x1 32.3 us: attend_back(): pl.pallas_call(functools.partial(attend_back_kernel, heads, key_block), o...]
    psum x1 -> x0, blocking collectives: 43.9 us -> none  [on_device(): lax.psum(attn_terms[0].astype(jnp.bfloat16), 'ctx').astype(jnp.float32)]
  transfers between devices with their start and end apart: 19 -> 127, of which waited for: 17 -> 65; matrix products, arithmetic and copies ran while one was open for 16% -> 17% of each run, Pallas kernels for 0% -> 12%
where the time goes in v1:
time: 465 us; the launch traced here: 455 us
  starting transfers between devices  162 us (35%)
  waiting for transfers between devices  155 us (33%)
  Pallas kernels  53.7 us (12%)
  matrix products  44.1 us (9%)
  other arithmetic  27.1 us (6%)
  local copies, waits for them, and re-layouts  10.8 us (2%)
    ppermute x69, starting transfers between devices, over_group(): return value if s == 0 else lax.ppermute(value, 'ctx', self.group_perm(s))  108 us
    ppermute x36, waiting for transfers between devices, over_rest(): return lax.ppermute(value, AXES, self.rest_perm(step))  83.6 us
    ppermute x69, waiting for transfers between devices, over_group(): return value if s == 0 else lax.ppermute(value, 'ctx', self.group_perm(s))  69.9 us
    ppermute x36, starting transfers between devices, over_rest(): return lax.ppermute(value, AXES, self.rest_perm(step))  51.8 us
    dot_general x35, matrix products, dotg(): lax.dot_general(a, b, (((ca,), (cb,)), ((), ())), preferred_element_type=...  44.1 us
    pallas_call x1, Pallas kernels, attend_back(): pl.pallas_call(functools.partial(attend_back_kernel, heads, key_block), o...  32.3 us
    pallas_call x1, Pallas kernels, attend(): pl.pallas_call(functools.partial(attend_kernel, heads, key_block), out_sh...  21.4 us
    convert_element_type x7, other arithmetic, sum_ctx(): return value.astype(F32)  10.8 us
  transfers between devices with their start and end apart: 127, of which 65 were waited for; matrix products, arithmetic and copies ran while one was open for 17% of the time, Pallas kernels for 12%

profile of v1, /device:TPU:0, one launch (start us, length us, event | category | flops | bytes accessed | tf_op | source)
XLA Modules:
  0.0 455.5 jit_solution(2432514078012679789)
XLA Ops:
  6.3 4.7 %collective-permute-start.12 = (bf16[192,256]{1,0:T(8,128)(2,1)S(1)}, bf16[192,256]{1,0:T(8,128)(2,1)S(1)}, u32[]{:S(2)}, u32[]{:S(2)}) collective-permute-start(bf16[192,256]{1,0:T(8,128)(2,1)S(1)} %get-tuple-element.152), channel_id=1, source_target_pairs={{0,12},{1,13},{2,14},{3,15},{4,8},{5,9},{6,10},{7,11},{8,4},{9,5},... | collective-permute-start | bytes 294920 | tf_op jit(solution)/shard_map/ppermute | solution.py:142
  16.9 4.8 %collective-permute-start.7 = (bf16[192,256]{1,0:T(8,128)(2,1)S(1)}, bf16[192,256]{1,0:T(8,128)(2,1)S(1)}, u32[]{:S(2)}, u32[]{:S(2)}) collective-permute-start(bf16[192,256]{1,0:T(8,128)(2,1)S(1)} %get-tuple-element.150), channel_id=1, source_target_pairs={{0,4},{1,5},{2,6},{3,7},{4,0},{5,1},{6,2},{7,3},{8,12},{9,13},{10,... | collective-permute-start | bytes 294920 | tf_op jit(solution)/shard_map/ppermute | solution.py:142
  21.7 5.1 %collective-permute-done.10 = bf16[192,256]{1,0:T(8,128)(2,1)S(1)} collective-permute-done((bf16[192,256]{1,0:T(8,128)(2,1)S(1)}, bf16[192,256]{1,0:T(8,128)(2,1)S(1)}, u32[]{:S(2)}, u32[]{:S(2)}) %collective-permute-start.10) | collective-permute-done | bytes 98336 | tf_op jit(solution)/shard_map/ppermute | solution.py:142
  32.8 14.3 %collective-permute-done.13.refs_1_ = bf16[384,1024]{1,0:T(8,128)(2,1)} collective-permute-done((bf16[384,1024]{1,0:T(8,128)(2,1)S(1)}, bf16[384,1024]{1,0:T(8,128)(2,1)}, u32[]{:S(2)}, u32[]{:S(2)}) %collective-permute-start.13) | collective-permute-done | bytes 786464 | tf_op jit(solution)/shard_map/ppermute | solution.py:139
  49.7 3.4 collective-permute-start.4
  63.8 21.4 %attend.1 = (f32[192,1024]{1,0:T(8,128)}, bf16[192,1024]{1,0:T(8,128)(2,1)}, f32[3,1024]{1,0:T(4,128)}) custom-call(bf16[192,1024]{1,0:T(8,128)(2,1)} %pad_maximum_fusion.q_ref, bf16[384,1024]{1,0:T(8,128)(2,1)} %copy-done.1, bf16[384,1024]{1,0:T(8,128)(2,1)} %collective-permute-done.13.refs_1_, bf16[384,1024]{1,0:T(8,128)(2,1)} %collective-permute-done.14.refs_2_, ...), custom_call_target="tpu_custom_call" | custom-call | tf_op jit(solution)/shard_map/attend/pallas_call | solution.py:58
  93.7 3.7 collective-permute-done.17
  102.9 10.9 %fusion.107 = f32[256,2048]{1,0:T(8,128)S(1)} fusion(bf16[256,384]{1,0:T(8,128)(2,1)S(1)} %get-tuple-element.141, bf16[384,2048]{1,0:T(8,128)(2,1)S(1)} %copy-done.4), kind=kOutput, calls=%fused_computation.431 | convolution fusion | flops 402653184 | bytes 3866624 | tf_op jit(solution)/shard_map/dot_general | solution.py:22
  131.8 2.9 fusion.21
  137.0 3.6 collective-permute-done.25
  143.0 32.3 %attend_back.1 = (bf16[192,1024]{1,0:T(8,128)(2,1)}, bf16[384,1024]{1,0:T(8,128)(2,1)}, bf16[384,1024]{1,0:T(8,128)(2,1)}, bf16[384,1024]{1,0:T(8,128)(2,1)}, bf16[384,1024]{1,0:T(8,128)(2,1)}) custom-call(bf16[192,1024]{1,0:T(8,128)(2,1)} %pad_maximum_fusion.q_ref, bf16[192,1024]{1,0:T(8,128)(2,1)} %pad_maximum_fusion.2.do_ref, ...), custom_call_target="tpu_custom_call" | custom-call | tf_op jit(solution)/shard_map/attend_back/pallas_call | solution.py:98
  184.0 3.1 collective-permute-done.28
  192.7 5.2 %collective-permute-done.82 = bf16[192,768]{1,0:T(8,128)(2,1)S(1)} collective-permute-done((bf16[192,768]{1,0:T(8,128)(2,1)S(1)}, bf16[192,768]{1,0:T(8,128)(2,1)S(1)}, u32[]{:S(2)}, u32[]{:S(2)}) %collective-permute-start.82) | collective-permute-done | bytes 294944 | tf_op jit(solution)/shard_map/ppermute | solution.py:139
  201.8 4.5 collective-permute-done.83
  224.2 10.0 %collective-permute-done.49 = bf16[96,768]{1,0:T(8,128)(2,1)S(1)} collective-permute-done((bf16[96,768]{1,0:T(8,128)(2,1)S(1)}, bf16[96,768]{1,0:T(8,128)(2,1)S(1)}, u32[]{:S(2)}, u32[]{:S(2)}) %collective-permute-start.49) | collective-permute-done | bytes 147488 | tf_op jit(solution)/shard_map/ppermute | solution.py:139
  247.3 3.0 collective-permute-start.53
  256.1 6.1 %collective-permute-done.56 = bf16[96,768]{1,0:T(8,128)(2,1)S(1)} collective-permute-done((bf16[96,768]{1,0:T(8,128)(2,1)S(1)}, bf16[96,768]{1,0:T(8,128)(2,1)S(1)}, u32[]{:S(2)}, u32[]{:S(2)}) %collective-permute-start.56) | collective-permute-done | bytes 147488 | tf_op jit(solution)/shard_map/ppermute | solution.py:139
  264.7 9.2 %collective-permute-done.91 = bf16[192,768]{1,0:T(8,128)(2,1)S(1)} collective-permute-done((bf16[192,768]{1,0:T(8,128)(2,1)S(1)}, bf16[192,768]{1,0:T(8,128)(2,1)S(1)}, u32[]{:S(2)}, u32[]{:S(2)}) %collective-permute-start.91) | collective-permute-done | bytes 294944 | tf_op jit(solution)/shard_map/ppermute | solution.py:139
  281.1 4.4 collective-permute-start.36
  288.2 4.2 collective-permute-start.121
  301.2 3.9 collective-permute-start.35
  314.1 4.3 collective-permute-start.41
  323.8 4.2 collective-permute-start.45
  329.6 3.8 collective-permute-start.122
  344.9 3.8 collective-permute-done.106
  348.7 2.9 collective-permute-start.97
  361.5 3.8 collective-permute-done.108
  375.2 3.1 collective-permute-done.110
  380.8 3.2 collective-permute-start.71
  384.3 3.5 collective-permute-done.71
  423.4 4.8 %collective-permute-done.113 = bf16[96,2048]{1,0:T(8,128)(2,1)S(1)} collective-permute-done((bf16[96,2048]{1,0:T(8,128)(2,1)S(1)}, bf16[96,2048]{1,0:T(8,128)(2,1)S(1)}, u32[]{:S(2)}, u32[]{:S(2)}) %collective-permute-start.113) | collective-permute-done | bytes 393248 | tf_op jit(solution)/shard_map/ppermute | solution.py:139
  437.3 9.1 %collective-permute-done.79 = bf16[192,768]{1,0:T(8,128)(2,1)S(1)} collective-permute-done((bf16[192,768]{1,0:T(8,128)(2,1)S(1)}, bf16[192,768]{1,0:T(8,128)(2,1)S(1)}, u32[]{:S(2)}, u32[]{:S(2)}) %collective-permute-start.79) | collective-permute-done | bytes 294944 | tf_op jit(solution)/shard_map/ppermute | solution.py:139
  (516 shorter events, 245.1 us)
Async XLA Ops:
  28.6 18.5 %collective-permute-start.13 = (bf16[384,1024]{1,0:T(8,128)(2,1)S(1)}, bf16[384,1024]{1,0:T(8,128)(2,1)}, u32[]{:S(2)}, u32[]{:S(2)}) collective-permute-start(bf16[384,1024]{1,0:T(8,128)(2,1)S(1)} %maximum_maximum_fusion.refs_0_), channel_id=1, source_target_pairs={{0,1},{1,0},{2,3},{3,2},{4,5},{5,4},{6,7},{7,6},{8,9},{9,8},{10,11... | collective-permute-start | bytes 2359304 | tf_op jit(solution)/shard_map/ppermute | solution.py:139
  30.2 18.4 %collective-permute-start.1 = (bf16[384,768]{1,0:T(8,128)(2,1)S(1)}, bf16[384,768]{1,0:T(8,128)(2,1)S(1)}, u32[]{:S(2)}, u32[]{:S(2)}) collective-permute-start(bf16[384,768]{1,0:T(8,128)(2,1)S(1)} %copy-done.28), channel_id=1, source_target_pairs={{0,16},{16,0},{1,17},{17,1},{2,18},{18,2},{3,19},{19,3},{4,20},{20... | collective-permute-start | bytes 1769480 | tf_op jit(solution)/shard_map/ppermute | solution.py:221
  30.2 58.5 %collective-permute-start.23 = (bf16[1024,768]{1,0:T(8,128)(2,1)S(1)}, bf16[1024,768]{1,0:T(8,128)(2,1)}, u32[]{:S(2)}, u32[]{:S(2)}) collective-permute-start(bf16[1024,768]{1,0:T(8,128)(2,1)S(1)} %copy-done.3), channel_id=1, source_target_pairs={{0,16},{16,0},{1,17},{17,1},{2,18},{18,2},{3,19},{19,3},{4,20},{20... | collective-permute-start | bytes 4718600 | tf_op jit(solution)/shard_map/ppermute | solution.py:221
  30.7 24.1 %collective-permute-start.20 = (bf16[384]{0:T(512)(128)(2,1)S(1)}, bf16[384]{0:T(512)(128)(2,1)}, u32[]{:S(2)}, u32[]{:S(2)}) collective-permute-start(bf16[384]{0:T(512)(128)(2,1)S(1)} %copy-done.38), channel_id=1, source_target_pairs={{0,16},{16,0},{1,17},{17,1},{2,18},{18,2},{3,19},{19,3},{4,20},{20... | collective-permute-start | bytes 2312 | tf_op jit(solution)/shard_map/ppermute | solution.py:221
  31.2 32.6 %collective-permute-start.14 = (bf16[384,1024]{1,0:T(8,128)(2,1)S(1)}, bf16[384,1024]{1,0:T(8,128)(2,1)}, u32[]{:S(2)}, u32[]{:S(2)}) collective-permute-start(bf16[384,1024]{1,0:T(8,128)(2,1)S(1)} %maximum_maximum_fusion.refs_0_), channel_id=1, source_target_pairs={{0,2},{1,3},{2,0},{3,1},{4,6},{5,7},{6,4},{7,5},{8,10},{9,11},{10,... | collective-permute-start | bytes 2359304 | tf_op jit(solution)/shard_map/ppermute | solution.py:139
  47.1 16.7 %collective-permute-start.15 = (bf16[384,1024]{1,0:T(8,128)(2,1)}, bf16[384,1024]{1,0:T(8,128)(2,1)}, u32[]{:S(2)}, u32[]{:S(2)}) collective-permute-start(bf16[384,1024]{1,0:T(8,128)(2,1)} %collective-permute-done.13.refs_1_), channel_id=1, source_target_pairs={{0,2},{1,3},{2,0},{3,1},{4,6},{5,7},{6,4},{7,5},{8,10},{9,11},{10,... | collective-permute-start | bytes 2359304 | tf_op jit(solution)/shard_map/ppermute | solution.py:139
  60.5 39.1 %collective-permute-start.19 = (bf16[384,768]{1,0:T(8,128)(2,1)S(1)}, bf16[384,768]{1,0:T(8,128)(2,1)}, u32[]{:S(2)}, u32[]{:S(2)}) collective-permute-start(bf16[384,768]{1,0:T(8,128)(2,1)S(1)} %copy-done.13), channel_id=1, source_target_pairs={{0,16},{16,0},{1,17},{17,1},{2,18},{18,2},{3,19},{19,3},{4,20},{20... | collective-permute-start | bytes 1769480 | tf_op jit(solution)/shard_map/ppermute | solution.py:221
  62.1 52.5 %collective-permute-start.22 = (bf16[384,2048]{1,0:T(8,128)(2,1)}, bf16[384,2048]{1,0:T(8,128)(2,1)}, u32[]{:S(2)}, u32[]{:S(2)}) collective-permute-start(bf16[384,2048]{1,0:T(8,128)(2,1)} %param.20), channel_id=1, source_target_pairs={{0,16},{16,0},{1,17},{17,1},{2,18},{18,2},{3,19},{19,3},{4,20},{20... | collective-permute-start | bytes 4718600 | tf_op jit(solution)/shard_map/ppermute | solution.py:221
  93.7 23.1 %collective-permute-start.21 = (bf16[384,2048]{1,0:T(8,128)(2,1)S(1)}, bf16[384,2048]{1,0:T(8,128)(2,1)S(1)}, u32[]{:S(2)}, u32[]{:S(2)}) collective-permute-start(bf16[384,2048]{1,0:T(8,128)(2,1)S(1)} %copy-done.2), channel_id=1, source_target_pairs={{0,16},{16,0},{1,17},{17,1},{2,18},{18,2},{3,19},{19,3},{4,20},{20... | collective-permute-start | bytes 4718600 | tf_op jit(solution)/shard_map/ppermute | solution.py:221
  97.5 93.0 %collective-permute-start.116 = (bf16[256,768]{1,0:T(8,128)(2,1)S(1)}, bf16[256,768]{1,0:T(8,128)(2,1)}, u32[]{:S(2)}, u32[]{:S(2)}) collective-permute-start(bf16[256,768]{1,0:T(8,128)(2,1)S(1)} %bitcast.95), channel_id=1, source_target_pairs={{0,16},{16,0},{1,17},{17,1},{2,18},{18,2},{3,19},{19,3},{4,20},{20... | collective-permute-start | bytes 1179656 | tf_op jit(solution)/shard_map/ppermute | solution.py:221
  125.6 53.2 %collective-permute-start.81 = (bf16[256,768]{1,0:T(8,128)(2,1)S(1)}, bf16[256,768]{1,0:T(8,128)(2,1)}, u32[]{:S(2)}, u32[]{:S(2)}) collective-permute-start(bf16[256,768]{1,0:T(8,128)(2,1)S(1)} %get-tuple-element.89), channel_id=1, source_target_pairs={{0,16},{16,0},{1,17},{17,1},{2,18},{18,2},{3,19},{19,3},{4,20},{20... | collective-permute-start | bytes 1179656 | tf_op jit(solution)/shard_map/ppermute | solution.py:221
  136.8 42.0 %collective-permute-start.80 = (bf16[384,256]{1,0:T(8,128)(2,1)}, bf16[384,256]{1,0:T(8,128)(2,1)S(1)}, u32[]{:S(2)}, u32[]{:S(2)}) collective-permute-start(bf16[384,256]{1,0:T(8,128)(2,1)} %get-tuple-element.142), channel_id=1, source_target_pairs={{0,16},{16,0},{1,17},{17,1},{2,18},{18,2},{3,19},{19,3},{4,20},{20... | collective-permute-start | bytes 589832 | tf_op jit(solution)/shard_map/ppermute | solution.py:221
  140.5 50.0 %collective-permute-start.115 = (bf16[256,1024]{1,0:T(8,128)(2,1)}, bf16[256,1024]{1,0:T(8,128)(2,1)}, u32[]{:S(2)}, u32[]{:S(2)}) collective-permute-start(bf16[256,1024]{1,0:T(8,128)(2,1)} %get-tuple-element.102), channel_id=1, source_target_pairs={{0,16},{16,0},{1,17},{17,1},{2,18},{18,2},{3,19},{19,3},{4,20},{20... | collective-permute-start | bytes 1572872 | tf_op jit(solution)/shard_map/ppermute | solution.py:221
  184.0 15.2 %collective-permute-start.46 = (bf16[256,384]{1,0:T(8,128)(2,1)S(1)}, bf16[256,384]{1,0:T(8,128)(2,1)S(1)}, u32[]{:S(2)}, u32[]{:S(2)}) collective-permute-start(bf16[256,384]{1,0:T(8,128)(2,1)S(1)} %copy-done.12), channel_id=1, source_target_pairs={{0,16},{16,0},{1,17},{17,1},{2,18},{18,2},{3,19},{19,3},{4,20},{20... | collective-permute-start | bytes 589832 | tf_op jit(solution)/shard_map/ppermute | solution.py:221
  187.1 30.3 %collective-permute-start.31 = (bf16[384,1024]{1,0:T(8,128)(2,1)S(1)}, bf16[384,1024]{1,0:T(8,128)(2,1)S(1)}, u32[]{:S(2)}, u32[]{:S(2)}) collective-permute-start(bf16[384,1024]{1,0:T(8,128)(2,1)S(1)} %copy-done.40), channel_id=1, source_target_pairs={{0,2},{1,3},{2,0},{3,1},{4,6},{5,7},{6,4},{7,5},{8,10},{9,11},{10,... | collective-permute-start | bytes 2359304 | tf_op jit(solution)/shard_map/ppermute | solution.py:139
  212.2 24.0 %collective-permute-start.93 = (bf16[256,2048]{1,0:T(8,128)(2,1)S(1)}, bf16[256,2048]{1,0:T(8,128)(2,1)S(1)}, u32[]{:S(2)}, u32[]{:S(2)}) collective-permute-start(bf16[256,2048]{1,0:T(8,128)(2,1)S(1)} %copy-done.6), channel_id=1, source_target_pairs={{0,16},{16,0},{1,17},{17,1},{2,18},{18,2},{3,19},{19,3},{4,20},{20... | collective-permute-start | bytes 3145736 | tf_op jit(solution)/shard_map/ppermute | solution.py:221
  213.6 21.1 %collective-permute-start.92 = (bf16[256,384]{1,0:T(8,128)(2,1)S(1)}, bf16[256,384]{1,0:T(8,128)(2,1)S(1)}, u32[]{:S(2)}, u32[]{:S(2)}) collective-permute-start(bf16[256,384]{1,0:T(8,128)(2,1)S(1)} %copy-done.21), channel_id=1, source_target_pairs={{0,16},{16,0},{1,17},{17,1},{2,18},{18,2},{3,19},{19,3},{4,20},{20... | collective-permute-start | bytes 589832 | tf_op jit(solution)/shard_map/ppermute | solution.py:221
  217.8 22.3 %collective-permute-start.104 = (bf16[256,2048]{1,0:T(8,128)(2,1)S(1)}, bf16[256,2048]{1,0:T(8,128)(2,1)S(1)}, u32[]{:S(2)}, u32[]{:S(2)}) collective-permute-start(bf16[256,2048]{1,0:T(8,128)(2,1)S(1)} %get-tuple-element.91), channel_id=1, source_target_pairs={{0,16},{16,0},{1,17},{17,1},{2,18},{18,2},{3,19},{19,3},{4,20},{20... | collective-permute-start | bytes 3145736 | tf_op jit(solution)/shard_map/ppermute | solution.py:221
  220.7 60.0 %collective-permute-start.30 = (bf16[384,1024]{1,0:T(8,128)(2,1)S(1)}, bf16[384,1024]{1,0:T(8,128)(2,1)S(1)}, u32[]{:S(2)}, u32[]{:S(2)}) collective-permute-start(bf16[384,1024]{1,0:T(8,128)(2,1)S(1)} %copy-done.39), channel_id=1, source_target_pairs={{0,2},{1,3},{2,0},{3,1},{4,6},{5,7},{6,4},{7,5},{8,10},{9,11},{10,... | collective-permute-start | bytes 2359304 | tf_op jit(solution)/shard_map/ppermute | solution.py:139
  234.2 30.0 %collective-permute-start.117 = (bf16[512,768]{1,0:T(8,128)(2,1)S(1)}, bf16[512,768]{1,0:T(8,128)(2,1)S(1)}, u32[]{:S(2)}, u32[]{:S(2)}) collective-permute-start(bf16[512,768]{1,0:T(8,128)(2,1)S(1)} %constant_dynamic-slice_fusion.4), channel_id=1, source_target_pairs={{0,1},{1,0},{2,3},{3,2},{4,5},{5,4},{6,7},{7,6},{8,9},{9,8},{10,11... | collective-permute-start | bytes 2359304 | tf_op jit(solution)/shard_map/ppermute | solution.py:139
  250.2 30.4 %collective-permute-start.32 = (bf16[384,1024]{1,0:T(8,128)(2,1)S(1)}, bf16[384,1024]{1,0:T(8,128)(2,1)S(1)}, u32[]{:S(2)}, u32[]{:S(2)}) collective-permute-start(bf16[384,1024]{1,0:T(8,128)(2,1)S(1)} %add_convert_fusion.4), channel_id=1, source_target_pairs={{0,1},{1,0},{2,3},{3,2},{4,5},{5,4},{6,7},{7,6},{8,9},{9,8},{10,11... | collective-permute-start | bytes 2359304 | tf_op jit(solution)/shard_map/ppermute | solution.py:139
  253.0 52.2 %collective-permute-start.94 = (bf16[192,2048]{1,0:T(8,128)(2,1)S(1)}, bf16[192,2048]{1,0:T(8,128)(2,1)S(1)}, u32[]{:S(2)}, u32[]{:S(2)}) collective-permute-start(bf16[192,2048]{1,0:T(8,128)(2,1)S(1)} %constant_dynamic-slice_fusion.14), channel_id=1, source_target_pairs={{0,1},{1,0},{2,3},{3,2},{4,5},{5,4},{6,7},{7,6},{8,9},{9,8},{10,11... | collective-permute-start | bytes 2359304 | tf_op jit(solution)/shard_map/ppermute | solution.py:139
  273.9 31.7 %collective-permute-start.105 = (bf16[192,2048]{1,0:T(8,128)(2,1)S(1)}, bf16[192,2048]{1,0:T(8,128)(2,1)S(1)}, u32[]{:S(2)}, u32[]{:S(2)}) collective-permute-start(bf16[192,2048]{1,0:T(8,128)(2,1)S(1)} %constant_dynamic-slice_fusion.9), channel_id=1, source_target_pairs={{0,1},{1,0},{2,3},{3,2},{4,5},{5,4},{6,7},{7,6},{8,9},{9,8},{10,11... | collective-permute-start | bytes 2359304 | tf_op jit(solution)/shard_map/ppermute | solution.py:139
  305.2 36.1 %collective-permute-start.69 = (bf16[768,256]{1,0:T(8,128)(2,1)S(1)}, bf16[768,256]{1,0:T(8,128)(2,1)S(1)}, u32[]{:S(2)}, u32[]{:S(2)}) collective-permute-start(bf16[768,256]{1,0:T(8,128)(2,1)S(1)} %pad_maximum_fusion.5), channel_id=1, source_target_pairs={{0,16},{16,0},{1,17},{17,1},{2,18},{18,2},{3,19},{19,3},{4,20},{20... | collective-permute-start | bytes 1179656 | tf_op jit(solution)/shard_map/ppermute | solution.py:221
  305.6 30.6 %collective-permute-start.124 = (bf16[64,768]{1,0:T(8,128)(2,1)S(1)}, bf16[64,768]{1,0:T(8,128)(2,1)S(1)}, u32[]{:S(2)}, u32[]{:S(2)}) collective-permute-start(bf16[64,768]{1,0:T(8,128)(2,1)S(1)} %add_convert_fusion.17), channel_id=1, source_target_pairs={{0,4},{1,5},{2,6},{3,7},{4,0},{5,1},{6,2},{7,3},{8,12},{9,13},{10,... | collective-permute-start | bytes 294920 | tf_op jit(solution)/shard_map/ppermute | solution.py:142
  336.2 15.5 %collective-permute-start.58 = (bf16[768,256]{1,0:T(8,128)(2,1)S(1)}, bf16[768,256]{1,0:T(8,128)(2,1)S(1)}, u32[]{:S(2)}, u32[]{:S(2)}) collective-permute-start(bf16[768,256]{1,0:T(8,128)(2,1)S(1)} %pad_maximum_fusion.4), channel_id=1, source_target_pairs={{0,16},{16,0},{1,17},{17,1},{2,18},{18,2},{3,19},{19,3},{4,20},{20... | collective-permute-start | bytes 1179656 | tf_op jit(solution)/shard_map/ppermute | solution.py:221
  341.9 38.8 %collective-permute-start.70 = (bf16[192,768]{1,0:T(8,128)(2,1)S(1)}, bf16[192,768]{1,0:T(8,128)(2,1)S(1)}, u32[]{:S(2)}, u32[]{:S(2)}) collective-permute-start(bf16[192,768]{1,0:T(8,128)(2,1)S(1)} %constant_dynamic-slice_fusion.24), channel_id=1, source_target_pairs={{0,1},{1,0},{2,3},{3,2},{4,5},{5,4},{6,7},{7,6},{8,9},{9,8},{10,11... | collective-permute-start | bytes 884744 | tf_op jit(solution)/shard_map/ppermute | solution.py:139
  358.3 33.7 %collective-permute-start.59 = (bf16[192,768]{1,0:T(8,128)(2,1)S(1)}, bf16[192,768]{1,0:T(8,128)(2,1)S(1)}, u32[]{:S(2)}, u32[]{:S(2)}) collective-permute-start(bf16[192,768]{1,0:T(8,128)(2,1)S(1)} %constant_dynamic-slice_fusion.29), channel_id=1, source_target_pairs={{0,1},{1,0},{2,3},{3,2},{4,5},{5,4},{6,7},{7,6},{8,9},{9,8},{10,11... | collective-permute-start | bytes 884744 | tf_op jit(solution)/shard_map/ppermute | solution.py:139
  374.8 60.5 %collective-permute-start.126 = (bf16[512,768]{1,0:T(8,128)(2,1)S(1)}, bf16[512,768]{1,0:T(8,128)(2,1)S(1)}, u32[]{:S(2)}, u32[]{:S(2)}) collective-permute-start(bf16[512,768]{1,0:T(8,128)(2,1)S(1)} %broadcast_select_fusion), channel_id=1, source_target_pairs={{0,1},{1,0},{2,3},{3,2},{4,5},{5,4},{6,7},{7,6},{8,9},{9,8},{10,11... | collective-permute-start | bytes 2359304 | tf_op jit(solution)/shard_map/ppermute | solution.py:139
  378.2 44.3 %collective-permute-start.102 = (bf16[96,2048]{1,0:T(8,128)(2,1)S(1)}, bf16[96,2048]{1,0:T(8,128)(2,1)S(1)}, u32[]{:S(2)}, u32[]{:S(2)}) collective-permute-start(bf16[96,2048]{1,0:T(8,128)(2,1)S(1)} %pad_maximum_fusion.8), channel_id=1, source_target_pairs={{0,2},{1,3},{2,0},{3,1},{4,6},{5,7},{6,4},{7,5},{8,10},{9,11},{10,... | collective-permute-start | bytes 1179656 | tf_op jit(solution)/shard_map/ppermute | solution.py:139
  422.8 27.9 %collective-permute-start.103 = (bf16[192,2048]{1,0:T(8,128)(2,1)S(1)}, bf16[192,2048]{1,0:T(8,128)(2,1)S(1)}, u32[]{:S(2)}, u32[]{:S(2)}) collective-permute-start(bf16[192,2048]{1,0:T(8,128)(2,1)S(1)} %broadcast_select_fusion.2), channel_id=1, source_target_pairs={{0,1},{1,0},{2,3},{3,2},{4,5},{5,4},{6,7},{7,6},{8,9},{9,8},{10,11... | collective-permute-start | bytes 2359304 | tf_op jit(solution)/shard_map/ppermute | solution.py:139
  428.4 24.5 %collective-permute-start.114 = (bf16[192,2048]{1,0:T(8,128)(2,1)S(1)}, bf16[192,2048]{1,0:T(8,128)(2,1)S(1)}, u32[]{:S(2)}, u32[]{:S(2)}) collective-permute-start(bf16[192,2048]{1,0:T(8,128)(2,1)S(1)} %broadcast_select_fusion.1), channel_id=1, source_target_pairs={{0,1},{1,0},{2,3},{3,2},{4,5},{5,4},{6,7},{7,6},{8,9},{9,8},{10,11... | collective-permute-start | bytes 2359304 | tf_op jit(solution)/shard_map/ppermute | solution.py:139
  (136 other events, 1149.9 us)
